TPU v7x, 32 devices: a whole 2x2x4 slice. The times are simulated.
32 devices in a mesh: ctx: 8 (over y, x, core), fsdp: 4 (over z).
Axes of the slice: x: 2, y: 2, z: 4, core: 2. Of those that a mesh axis runs over, the one named last changes fastest.
Arguments:
- loaded: bfloat16 [8, 8, 128, 4096], P('ctx', None, None, 'fsdp'), may hold values from -6 to 6
- slot_pos: int32 [8, 8, 128], P('ctx'), may hold values from -1 to 255, as said below
- contig_lengths: int32 [16], replicated, may hold values from 1 to 1024, 2048 in all
- w_in: bfloat16 [4096, 3, 4096], P('ctx', None, 'fsdp'), may hold values from -0.09375 to 0.09375
- short_taps: float32 [3, 7, 4096], P(None, None, 'fsdp'), may hold values from -2 to 2
- long_taps: float32 [128, 4096], P(None, 'fsdp'), may hold values from -0.5 to 0.5
- grad_out: bfloat16 [2048, 4096], P('ctx', 'fsdp'), may hold values from -0.59765625 to 0.59765625
Outputs:
- gated_out: bfloat16 [2048, 4096], P('ctx', 'fsdp')
- token_grads: bfloat16 [2048, 4096], P('ctx', 'fsdp')
- weight_grads: bfloat16 [4096, 3, 4096], P('ctx', None, 'fsdp')
- short_grads: float32 [3, 7, 4096], P(None, None, 'fsdp')
- long_grads: float32 [128, 4096], P(None, 'fsdp')
Inputs may be any that keep to these rules, and one draw needn't show every extreme that they name: `slot_pos`: for each destination e, the slots with a value of 0 or more name every row 0 to 255 of e's block exactly once; -1 marks an empty slot; for each destination some loader fills all 128 of its slots. `contig_lengths`: the lengths sum to 2048.
All inputs are finite; a program needn't handle non-finite values.
Results may differ from a plain program's by a relative error of at most 0.012.
Values may be sent and summed in bfloat16 or wider, within the bound.
A program may use at most 192 MiB of HBM per device.

v0:
```python
import jax
import jax.numpy as jnp
from jax import lax
from jax.sharding import PartitionSpec as P


def passed_along(x, axis, by):
    size = lax.axis_size(axis)
    pairs = [(i, i + by) for i in range(size) if 0 <= i + by < size]
    return lax.ppermute(x, axis, pairs)


def starts_of(positions, contig_lengths):
    ends = jnp.cumsum(contig_lengths, dtype=jnp.int32)
    begins = ends - contig_lengths
    chosen = jnp.where(begins[None, :] <= positions[:, None], begins[None, :], 0)
    return jnp.max(chosen, axis=1)


def lead_filter(ext, taps, positions, begins_here):
    width = taps.shape[0]
    count = ext.shape[0] - width + 1
    bcast_shape = (count,) + (1,) * (ext.ndim - 1)
    total = jnp.zeros((count,) + ext.shape[1:], jnp.float32)
    for tap_index in range(width):
        keep_mask = (positions - tap_index >= begins_here).astype(jnp.float32).reshape(bcast_shape)
        first = width - 1 - tap_index
        total = total + taps[tap_index] * ext[first : first + count] * keep_mask
    return total


def trail_filter(ext, taps, positions, begins_ext):
    width = taps.shape[0]
    count = ext.shape[0] - width + 1
    bcast_shape = (count,) + (1,) * (ext.ndim - 1)
    total = jnp.zeros((count,) + ext.shape[1:], jnp.float32)
    for tap_index in range(width):
        keep_mask = (
            (positions >= begins_ext[tap_index : tap_index + count])
            .astype(jnp.float32)
            .reshape(bcast_shape)
        )
        total = total + taps[tap_index] * ext[tap_index : tap_index + count] * keep_mask
    return total


def tap_sums(grads, ext, width, lead_count, positions, begins_here):
    count = grads.shape[0]
    bcast_shape = (count,) + (1,) * (grads.ndim - 1)
    pieces = []
    for tap_index in range(width):
        keep_mask = (positions - tap_index >= begins_here).astype(jnp.float32).reshape(bcast_shape)
        first = lead_count - tap_index
        pieces.append(jnp.sum(grads * ext[first : first + count] * keep_mask, axis=0))
    return jnp.stack(pieces, 0)


def on_device(loaded, slot_pos, contig_lengths, w_in, short_taps, long_taps, grad_out):
    moved = lax.all_to_all(loaded, "ctx", split_axis=1, concat_axis=0, tiled=True)
    feat_cols = moved.shape[3]
    slot_rows = moved.reshape(-1, feat_cols)
    tok_rows = grad_out.shape[0]
    short_width = short_taps.shape[1]
    long_width = long_taps.shape[0]
    targets = slot_pos.reshape(-1)
    picker = (targets[None, :] == jnp.arange(tok_rows, dtype=jnp.int32)[:, None]).astype(
        jnp.bfloat16
    )
    own_part = jnp.dot(picker, slot_rows, preferred_element_type=jnp.float32).astype(jnp.bfloat16)
    tokens = lax.all_gather(own_part, "fsdp", axis=1, tiled=True)
    gathered = lax.all_gather(w_in, "ctx", axis=0, tiled=True)
    streams = jnp.einsum("td,dsc->tsc", tokens, gathered, preferred_element_type=jnp.float32)
    proj_half = streams.astype(jnp.bfloat16)
    offset = lax.axis_index("ctx") * tok_rows
    positions = offset + jnp.arange(tok_rows, dtype=jnp.int32)
    begins_here = starts_of(positions, contig_lengths)
    short_lags = jnp.transpose(short_taps, (1, 0, 2))
    prev_rows = passed_along(proj_half[tok_rows - (short_width - 1) :], "ctx", 1)
    lead_mixed = jnp.concatenate([prev_rows, proj_half], 0).astype(jnp.float32)
    lead_count = short_width - 1
    filtered = lead_filter(lead_mixed, short_lags, positions, begins_here)
    product = (filtered[:, 1] * filtered[:, 2]).astype(jnp.bfloat16)
    prior_rows = passed_along(product[tok_rows - (long_width - 1) :], "ctx", 1)
    lead_product = jnp.concatenate([prior_rows, product], 0).astype(jnp.float32)
    carried = lead_filter(lead_product, long_taps, positions, begins_here)
    gated_out = (filtered[:, 0] * carried).astype(jnp.bfloat16)
    upstream = grad_out.astype(jnp.float32)
    back_prod = (upstream * filtered[:, 0]).astype(jnp.bfloat16)
    first_grad = upstream * carried
    next_rows = passed_along(back_prod[: long_width - 1], "ctx", -1)
    long_begins = starts_of(
        offset + jnp.arange(tok_rows + long_width - 1, dtype=jnp.int32), contig_lengths
    )
    trail_prod = jnp.concatenate([back_prod, next_rows], 0).astype(jnp.float32)
    grad_product = trail_filter(trail_prod, long_taps, positions, long_begins)
    grad_filtered = jnp.stack(
        [first_grad, grad_product * filtered[:, 2], grad_product * filtered[:, 1]], 1
    ).astype(jnp.bfloat16)
    next_grads = passed_along(grad_filtered[: short_width - 1], "ctx", -1)
    short_begins = starts_of(
        offset + jnp.arange(tok_rows + short_width - 1, dtype=jnp.int32), contig_lengths
    )
    trail_grad = jnp.concatenate([grad_filtered, next_grads], 0).astype(jnp.float32)
    grad_mixed = trail_filter(trail_grad, short_lags, positions, short_begins).astype(jnp.bfloat16)
    long_local = tap_sums(
        back_prod.astype(jnp.float32),
        lead_product,
        long_width,
        long_width - 1,
        positions,
        begins_here,
    )
    short_local = tap_sums(
        grad_filtered.astype(jnp.float32),
        lead_mixed,
        short_width,
        lead_count,
        positions,
        begins_here,
    )
    short_total, long_total = (
        lax.psum(jnp.transpose(short_local, (1, 0, 2)).astype(jnp.bfloat16), "ctx").astype(
            jnp.float32
        ),
        lax.psum(long_local.astype(jnp.bfloat16), "ctx").astype(jnp.float32),
    )
    partial_value = jnp.einsum(
        "tsc,dsc->td", grad_mixed, gathered, preferred_element_type=jnp.float32
    )
    token_grads = lax.psum_scatter(
        partial_value.astype(jnp.bfloat16), "fsdp", scatter_dimension=1, tiled=True
    )
    weight_grads = lax.psum_scatter(
        jnp.einsum("td,tsc->dsc", tokens, grad_mixed, preferred_element_type=jnp.float32).astype(
            jnp.bfloat16
        ),
        "ctx",
        scatter_dimension=0,
        tiled=True,
    )
    return (gated_out, token_grads, weight_grads, short_total, long_total)


def solution(mesh):
    in_specs = (
        P("ctx", None, None, "fsdp"),
        P("ctx", None, None),
        P(),
        P("ctx", None, "fsdp"),
        P(None, None, "fsdp"),
        P(None, "fsdp"),
        P("ctx", "fsdp"),
    )
    out_specs = (
        P("ctx", "fsdp"),
        P("ctx", "fsdp"),
        P("ctx", None, "fsdp"),
        P(None, None, "fsdp"),
        P(None, "fsdp"),
    )
    return jax.shard_map(
        on_device, mesh=mesh, in_specs=in_specs, out_specs=out_specs, check_vma=False
    )
```

profile of v0, /device:TPU:0, one launch (start us, length us, event | category | flops | bytes accessed | tf_op | source)
XLA Modules:
  0.0 702.3 jit_solution(11985297371757299991)
XLA Ops:
  7.2 31.8 %all_to_all.4 = bf16[1,8,128,1024]{3,2,0,1:T(8,128)(2,1)S(1)} all-to-all(bf16[1,8,128,1024]{3,2,0,1:T(8,128)(2,1)} %bitcast.209), channel_id=1, replica_groups=mesh['ctx'=8,'fsdp'=4] {'ctx'}, dimensions={1} | all-to-all | bytes 4194304 | tf_op jit(solution)/shard_map/all_to_all | solution.py:59
  53.0 33.0 %all-gather.3.cloned.1.call-done = bf16[256,4096]{1,0:T(8,128)(2,1)} async-done(((bf16[256,1024]{1,0:T(8,128)(2,1)}), bf16[256,4096]{1,0:T(8,128)(2,1)}) %all-gather.3.cloned.1.call-update) | async-done | bytes 2097168 | tf_op jit(solution)/shard_map/all_gather | solution.py:70
  86.0 126.0 %all-gather.5.cloned.1.call-done = bf16[4096,3,1024]{2,0,1:T(8,128)(2,1)} async-done(((bf16[512,3,1024]{2,0,1:T(8,128)(2,1)}), bf16[4096,3,1024]{2,0,1:T(8,128)(2,1)}) %all-gather.5.cloned.1.call-update) | async-done | bytes 25165840 | tf_op jit(solution)/shard_map/all_gather | solution.py:71
  212.0 12.2 %fusion.32 = bf16[256,3,1024]{2,0,1:T(8,128)(2,1)S(1)} fusion(bf16[4096,3,1024]{2,0,1:T(8,128)(2,1)} %all-gather.5.cloned.1.call-done, bf16[256,4096]{1,0:T(8,128)(2,1)} %all-gather.3.cloned.1.call-done), kind=kOutput, calls=%fused_computation.177 | convolution fusion | flops 6443237376 | bytes 28835840 | tf_op jit(solution)/shard_map/td,dsc->tsc/dot_general | solution.py:72
  227.8 3.6 multiply_add_fusion
  231.7 3.7 collective-permute-start.1
  237.0 3.4 fusion.266
  242.6 3.3 fusion.268
  245.9 3.3 fusion.270
  249.2 3.3 fusion.272
  252.5 3.3 fusion.274
  258.9 3.3 fusion.278
  262.1 3.3 fusion.280
  265.4 3.3 fusion.282
  268.8 3.3 fusion.284
  272.1 3.3 fusion.286
  275.5 3.5 fusion.288
  279.3 3.3 fusion.290
  283.0 9.1 %multiply_add_fusion.2 = f32[256,1024]{1,0:T(8,128)S(1)} fusion(f32[383,1024]{1,0:T(8,128)S(1)} %maximum_convert_fusion.2, f32[256]{0:T(256)} %copy-done.108, f32[1024]{0:T(1024)S(1)} %bitcast.309, f32[256]{0:T(256)} %copy-done.109, f32[1024]{0:T(1024)S(1)} %bitcast.312, f32[256]{0:T(256)} %copy-done.110, f32[1024]{0:T(1024)S(1)} %bitcast.314, ...), kind=kLoop, calls=%fused_computation.832 | loop fusion | flops 33554432 | bytes 46357504 | tf_op jit(solution)/shard_map/add | solution.py:28
  292.1 19.1 %fusion.550 = (bf16[256,1,1024]{2,0,1:T(8,128)(2,1)}, f32[256,1024]{1,0:T(8,128)}) fusion(bf16[256,1024]{1,0:T(8,128)(2,1)} %param.13, f32[256]{0:T(256)} %get-tuple-element.435, f32[383,1024]{1,0:T(8,128)S(1)} %maximum_convert_fusion.2, f32[1024]{0:T(1024)} %bitcast.279, f32[256]{0:T(256)} %get-tuple-element.436, f32[1024]{0:T(1024)} %bitcast.281, ...), kind=kLoop, calls=%fused_computation.840 | loop fusion | flops 67633152 | bytes 92709888 | tf_op jit(solution)/shard_map/stack | solution.py:96
  316.3 8.4 %fusion.486 = f32[256,1024]{1,0:T(8,128)} fusion(f32[383,1024]{1,0:T(8,128)S(1)} %maximum_convert_fusion.3, f32[256]{0:T(256)} %get-tuple-element.407, f32[256]{0:T(256)} %get-tuple-element.408, f32[256]{0:T(256)} %get-tuple-element.409, f32[256]{0:T(256)} %get-tuple-element.410, f32[256]{0:T(256)} %get-tuple-element.411, f32[256]{0:T(256)} %get-tuple-element.412, ...), kind=kLoop, calls=%fused_computation.732 | loop fusion | flops 24903680 | bytes 34766848 | tf_op jit(solution)/shard_map/add | solution.py:43
  324.8 25.0 %fusion.548 = (bf16[256,1,1024]{2,0,1:T(8,128)(2,1)}, f32[256,1024]{1,0:T(8,128)}) fusion(f32[256,3,1024]{2,0,1:T(8,128)} %copy-done.4, f32[256]{0:T(256)} %get-tuple-element.307, f32[383,1024]{1,0:T(8,128)S(1)} %maximum_convert_fusion.3, f32[1024]{0:T(1024)S(1)} %bitcast.280, f32[256]{0:T(256)} %get-tuple-element.308, f32[1024]{0:T(1024)S(1)} %bitcast.282, ...), kind=kLoop, calls=%fused_computation.838 | loop fusion | flops 76021760 | bytes 104824832 | tf_op jit(solution)/shard_map/stack | solution.py:96
  349.9 3.4 fusion.549
  416.0 10.6 %stack.704 = bf16[128,1024]{1,0:T(8,128)(2,1)} concatenate(bf16[1,1024]{1,0:T(2,128)(2,1)S(1)} %stack.576, bf16[1,1024]{1,0:T(2,128)(2,1)S(1)} %stack.577, bf16[1,1024]{1,0:T(2,128)(2,1)S(1)} %stack.578, bf16[1,1024]{1,0:T(2,128)(2,1)S(1)} %stack.579, bf16[1,1024]{1,0:T(2,128)(2,1)S(1)} %stack.580, bf16[1,1024]{1,0:T(2,128)(2,1)S(1)} %stack.581, bf16[1,1024]{1,0:T(2,128)(2,1)S(1)} %stack.582, ...), dimensions={0} | concatenate | bytes 524288 | tf_op jit(solution)/shard_map/stack | solution.py:55
  427.2 3.9 fusion.17
  431.0 13.2 %fusion = bf16[256,4096]{1,0:T(8,128)(2,1)} fusion(bf16[256,3,1024]{2,0,1:T(8,128)(2,1)S(1)} %fusion.17, bf16[4096,3,1024]{2,0,1:T(8,128)(2,1)} %all-gather.5.cloned.1.call-done), kind=kOutput, calls=%fused_computation.137 | convolution fusion | flops 6443499520 | bytes 28835840 | tf_op jit(solution)/shard_map/tsc,dsc->td/dot_general | solution.py:127
  444.3 13.5 %convolution_convert_fusion = bf16[4096,3,1024]{2,0,1:T(8,128)(2,1)} fusion(bf16[256,3,1024]{2,0,1:T(8,128)(2,1)S(1)} %fusion.17, bf16[256,4096]{1,0:T(8,128)(2,1)} %all-gather.3.cloned.1.call-done), kind=kOutput, calls=%fused_computation.128 | convolution fusion | flops 6455033856 | bytes 28835840 | tf_op jit(solution)/shard_map/td,tsc->dsc/dot_general | solution.py:134
  457.8 31.4 %all-reduce.2.cloned.1.call-done = bf16[128,1024]{1,0:T(8,128)(2,1)} async-done(((bf16[128,1024]{1,0:T(8,128)(2,1)}), bf16[128,1024]{1,0:T(8,128)(2,1)}) %all-reduce.2.cloned.1.call-update) | async-done | bytes 262160 | tf_op jit(solution)/shard_map/psum | solution.py:125
  493.3 3.7 fusion.14
  497.1 23.5 %psum.14 = bf16[3,7,1024]{2,0,1:T(4,128)(2,1)S(1)} all-reduce(bf16[3,7,1024]{2,0,1:T(4,128)(2,1)S(1)} %bitcast.214), channel_id=1, replica_groups=mesh['ctx'=8,'fsdp'=4] {'ctx'}, use_global_device_ids=true, to_apply=%region_13.14 | all-reduce | flops 21504 | bytes 86016 | tf_op jit(solution)/shard_map/psum | solution.py:122
  521.3 14.0 %reduce-scatter.3.cloned.1.call-done = bf16[256,1024]{1,0:T(8,128)(2,1)} async-done(((bf16[256,4096]{1,0:T(8,128)(2,1)}), bf16[256,1024]{1,0:T(8,128)(2,1)}) %reduce-scatter.3.cloned.1.call-update) | async-done | bytes 524304 | tf_op jit(solution)/shard_map/reduce_scatter | solution.py:130
  535.3 160.2 %reduce-scatter.5.cloned.1.call-done = bf16[512,3,1024]{2,0,1:T(8,128)(2,1)} async-done(((bf16[4096,3,1024]{2,0,1:T(8,128)(2,1)}), bf16[512,3,1024]{2,0,1:T(8,128)(2,1)}) %reduce-scatter.5.cloned.1.call-update) | async-done | bytes 3145744 | tf_op jit(solution)/shard_map/reduce_scatter | solution.py:133
  (571 shorter events, 96.0 us)
Async XLA Ops:
  7.2 78.8 %all-gather.3.cloned.1.call-start = ((), (), s32[]{:S(2)}) async-start(), calls=%async_computation.3 | async-start | bytes 2621440 | tf_op jit(solution)/shard_map/all_gather | solution.py:70
  40.6 171.5 %all-gather.5.cloned.1.call-start = ((), (), s32[]{:S(2)}) async-start(), calls=%async_computation.4 | async-start | bytes 28311552 | tf_op jit(solution)/shard_map/all_gather | solution.py:71
  41.3 447.9 %all-reduce.2.cloned.1.call-start = ((), (), s32[]{:S(2)}) async-start(), calls=%async_computation.7 | async-start | bytes 524288 | tf_op jit(solution)/shard_map/psum | solution.py:125
  52.8 216.0 %copy-start.110 = (f32[256]{0:T(256)}, f32[256]{0:T(256)S(1)}, u32[]{:S(2)}) copy-start(f32[256]{0:T(256)S(1)} %get-tuple-element.521) | copy-start | bytes 3076
  52.8 215.9 %copy-start.111 = (f32[256]{0:T(256)}, f32[256]{0:T(256)S(1)}, u32[]{:S(2)}) copy-start(f32[256]{0:T(256)S(1)} %get-tuple-element.522) | copy-start | bytes 3076
  52.8 215.9 %copy-start.112 = (f32[256]{0:T(256)}, f32[256]{0:T(256)S(1)}, u32[]{:S(2)}) copy-start(f32[256]{0:T(256)S(1)} %get-tuple-element.523) | copy-start | bytes 3076
  52.8 215.9 %copy-start.113 = (f32[256]{0:T(256)}, f32[256]{0:T(256)S(1)}, u32[]{:S(2)}) copy-start(f32[256]{0:T(256)S(1)} %get-tuple-element.524) | copy-start | bytes 3076
  52.8 219.2 %copy-start.118 = (f32[256]{0:T(256)}, f32[256]{0:T(256)S(1)}, u32[]{:S(2)}) copy-start(f32[256]{0:T(256)S(1)} %get-tuple-element.529) | copy-start | bytes 3076
  52.8 219.2 %copy-start.119 = (f32[256]{0:T(256)}, f32[256]{0:T(256)S(1)}, u32[]{:S(2)}) copy-start(f32[256]{0:T(256)S(1)} %get-tuple-element.530) | copy-start | bytes 3076
  52.9 219.2 %copy-start.120 = (f32[256]{0:T(256)}, f32[256]{0:T(256)S(1)}, u32[]{:S(2)}) copy-start(f32[256]{0:T(256)S(1)} %get-tuple-element.531) | copy-start | bytes 3076
  52.9 219.2 %copy-start.121 = (f32[256]{0:T(256)}, f32[256]{0:T(256)S(1)}, u32[]{:S(2)}) copy-start(f32[256]{0:T(256)S(1)} %get-tuple-element.532) | copy-start | bytes 3076
  52.9 219.2 %copy-start.122 = (f32[256]{0:T(256)}, f32[256]{0:T(256)S(1)}, u32[]{:S(2)}) copy-start(f32[256]{0:T(256)S(1)} %get-tuple-element.533) | copy-start | bytes 3076
  52.9 219.2 %copy-start.123 = (f32[256]{0:T(256)}, f32[256]{0:T(256)S(1)}, u32[]{:S(2)}) copy-start(f32[256]{0:T(256)S(1)} %get-tuple-element.534) | copy-start | bytes 3076
  52.9 219.2 %copy-start.124 = (f32[256]{0:T(256)}, f32[256]{0:T(256)S(1)}, u32[]{:S(2)}) copy-start(f32[256]{0:T(256)S(1)} %get-tuple-element.535) | copy-start | bytes 3076
  52.9 219.2 %copy-start.125 = (f32[256]{0:T(256)}, f32[256]{0:T(256)S(1)}, u32[]{:S(2)}) copy-start(f32[256]{0:T(256)S(1)} %get-tuple-element.536) | copy-start | bytes 3076
  52.9 222.5 %copy-start.126 = (f32[256]{0:T(256)}, f32[256]{0:T(256)S(1)}, u32[]{:S(2)}) copy-start(f32[256]{0:T(256)S(1)} %get-tuple-element.537) | copy-start | bytes 3076
  52.9 222.5 %copy-start.127 = (f32[256]{0:T(256)}, f32[256]{0:T(256)S(1)}, u32[]{:S(2)}) copy-start(f32[256]{0:T(256)S(1)} %get-tuple-element.538) | copy-start | bytes 3076
  52.9 222.5 %copy-start.128 = (f32[256]{0:T(256)}, f32[256]{0:T(256)S(1)}, u32[]{:S(2)}) copy-start(f32[256]{0:T(256)S(1)} %get-tuple-element.539) | copy-start | bytes 3076
  52.9 222.5 %copy-start.129 = (f32[256]{0:T(256)}, f32[256]{0:T(256)S(1)}, u32[]{:S(2)}) copy-start(f32[256]{0:T(256)S(1)} %get-tuple-element.540) | copy-start | bytes 3076
  53.0 222.5 %copy-start.130 = (f32[256]{0:T(256)}, f32[256]{0:T(256)S(1)}, u32[]{:S(2)}) copy-start(f32[256]{0:T(256)S(1)} %get-tuple-element.541) | copy-start | bytes 3076
  53.0 222.5 %copy-start.131 = (f32[256]{0:T(256)}, f32[256]{0:T(256)S(1)}, u32[]{:S(2)}) copy-start(f32[256]{0:T(256)S(1)} %get-tuple-element.542) | copy-start | bytes 3076
  53.0 222.5 %copy-start.132 = (f32[256]{0:T(256)}, f32[256]{0:T(256)S(1)}, u32[]{:S(2)}) copy-start(f32[256]{0:T(256)S(1)} %get-tuple-element.543) | copy-start | bytes 3076
  53.0 222.5 %copy-start.133 = (f32[256]{0:T(256)}, f32[256]{0:T(256)S(1)}, u32[]{:S(2)}) copy-start(f32[256]{0:T(256)S(1)} %get-tuple-element.544) | copy-start | bytes 3076
  53.0 225.9 %copy-start.134 = (f32[256]{0:T(256)}, f32[256]{0:T(256)S(1)}, u32[]{:S(2)}) copy-start(f32[256]{0:T(256)S(1)} %get-tuple-element.545) | copy-start | bytes 3076
  53.0 225.9 %copy-start.135 = (f32[256]{0:T(256)}, f32[256]{0:T(256)S(1)}, u32[]{:S(2)}) copy-start(f32[256]{0:T(256)S(1)} %get-tuple-element.546) | copy-start | bytes 3076
  53.0 225.9 %copy-start.136 = (f32[256]{0:T(256)}, f32[256]{0:T(256)S(1)}, u32[]{:S(2)}) copy-start(f32[256]{0:T(256)S(1)} %get-tuple-element.547) | copy-start | bytes 3076
  224.2 3.0 collective-permute-start
  231.7 5.0 collective-permute-start.1
  241.2 73.5 %collective-permute-start.2 = (bf16[127,1024]{1,0:T(8,128)(2,1)}, bf16[127,1024]{1,0:T(8,128)(2,1)S(1)}, u32[]{:S(2)}, u32[]{:S(2)}) collective-permute-start(bf16[127,1024]{1,0:T(8,128)(2,1)} %slice.2608), channel_id=1, source_target_pairs={{4,0},{8,4},{12,8},{16,12},{20,16},{24,20},{28,24},{5,1},{9,5},{13... | collective-permute-start | bytes 780296 | tf_op jit(solution)/shard_map/ppermute | solution.py:10
  353.9 72.8 %collective-permute-start.3 = (bf16[6,3,1024]{2,0,1:T(8,128)(2,1)S(1)}, bf16[6,3,1024]{2,0,1:T(8,128)(2,1)S(1)}, u32[]{:S(2)}, u32[]{:S(2)}) collective-permute-start(bf16[6,3,1024]{2,0,1:T(8,128)(2,1)S(1)} %slice.2737), channel_id=1, source_target_pairs={{4,0},{8,4},{12,8},{16,12},{20,16},{24,20},{28,24},{5,1},{9,5},{13... | collective-permute-start | bytes 110600 | tf_op jit(solution)/shard_map/ppermute | solution.py:10
  426.6 108.7 %reduce-scatter.3.cloned.1.call-start = ((), (), s32[]{:S(2)}) async-start(), calls=%async_computation.5 | async-start | bytes 2621440 | tf_op jit(solution)/shard_map/reduce_scatter | solution.py:130
  444.2 251.3 %reduce-scatter.5.cloned.1.call-start = ((), (), s32[]{:S(2)}) async-start(), calls=%async_computation.6 | async-start | bytes 28311552 | tf_op jit(solution)/shard_map/reduce_scatter | solution.py:133
  (162 other events, 5792.6 us)
Sparse Core Ops, SparseCore 0:
  40.7 45.3 all-gather.2
  87.9 124.0 all-gather.4
  426.8 62.3 all-reduce.1
  492.0 43.2 reduce-scatter.2
  539.4 156.1 reduce-scatter.4
where the time goes:
time: 712 us; the launch traced here: 702 us
  waiting for transfers between devices  366 us (51%)
  other arithmetic  137 us (19%)
  local copies, waits for them, and re-layouts  77.5 us (11%)
  blocking collectives  55.3 us (8%)
  matrix products  40.3 us (6%)
  between operations  17.3 us (2%)
  starting transfers between devices  8.79 us (1%)
    reduce_scatter x1, waiting for transfers between devices, on_device(): lax.psum_scatter(jnp.einsum('td,tsc->dsc', tokens, grad_mixed, preferred_...  160 us
    all_gather x1, waiting for transfers between devices, on_device(): gathered = lax.all_gather(w_in, 'ctx', axis=0, tiled=True)  126 us
    another operation x130, local copies, waits for them, and re-layouts, tap_sums(): return jnp.stack(pieces, 0)  70.2 us
    reduce_sum x17, other arithmetic, tap_sums(): pieces.append(jnp.sum(grads * ext[first:first + count] * keep_mask, axis=0))  52.3 us
    another operation x4, other arithmetic, on_device(): jnp.stack([first_grad, grad_product * filtered[:, 2], grad_product * filt...  47.6 us
    all_gather x1, waiting for transfers between devices, on_device(): tokens = lax.all_gather(own_part, 'fsdp', axis=1, tiled=True)  33 us
    all_to_all x1, blocking collectives, on_device(): lax.all_to_all(loaded, 'ctx', split_axis=1, concat_axis=0, tiled=True)  31.8 us
    psum x1, waiting for transfers between devices, on_device(): lax.psum(long_local.astype(jnp.bfloat16), 'ctx').astype(jnp.float32)  31.4 us
  transfers between devices with their start and end apart: 9, of which 6 were waited for; matrix products, arithmetic and copies ran while one was open for 28% of the time, Pallas kernels for 0%

commit v1 on v0

--- a/solution.py
+++ b/solution.py
@@ -67,7 +67,12 @@
         jnp.bfloat16
     )
     own_part = jnp.dot(picker, slot_rows, preferred_element_type=jnp.float32).astype(jnp.bfloat16)
-    tokens = lax.all_gather(own_part, "fsdp", axis=1, tiled=True)
+    ring = [own_part]
+    for hop in range(3):
+        ring.append(lax.ppermute(ring[-1], "fsdp", [(dev, (dev + 1) % 4) for dev in range(4)]))
+    tokens = jnp.roll(
+        jnp.concatenate(ring[::-1], axis=1), (lax.axis_index("fsdp") + 1) * ring[0].shape[1], axis=1
+    )
     gathered = lax.all_gather(w_in, "ctx", axis=0, tiled=True)
     streams = jnp.einsum("td,dsc->tsc", tokens, gathered, preferred_element_type=jnp.float32)
     proj_half = streams.astype(jnp.bfloat16)

time: 712 us -> 651 us (0.914)
  waiting for transfers between devices: 366 us -> 322 us
  blocking collectives: 55.3 us -> 23.7 us
  starting transfers between devices: 8.79 us -> 17.1 us
    all_gather x1, waiting for transfers between devices: 126 us -> 54.6 us  [on_device(): gathered = lax.all_gather(w_in, 'ctx', axis=0, tiled=True)]
    all_to_all x0 -> x1, waiting for transfers between devices: none -> 34 us  [on_device(): lax.all_to_all(loaded, 'ctx', split_axis=1, concat_axis=0, tiled=True)]
    all_gather x1 -> x0, waiting for transfers between devices: 33 us -> none  [on_device(): tokens = lax.all_gather(own_part, 'fsdp', axis=1, tiled=True)]
    all_to_all x1 -> x0, blocking collectives: 31.8 us -> none  [on_device(): lax.all_to_all(loaded, 'ctx', split_axis=1, concat_axis=0, tiled=True)]
    ppermute x0 -> x3, waiting for transfers between devices: none -> 26.8 us  [on_device(): lax.ppermute(ring[-1], 'fsdp', [(dev, (dev + 1) % 4) for dev in range(4)])]
  transfers between devices with their start and end apart: 9 -> 12, of which waited for: 6 -> 9; matrix products, arithmetic and copies ran while one was open for 28% -> 31% of each run, Pallas kernels for 0% -> 0%
where the time goes in v1:
time: 651 us; the launch traced here: 641 us
  waiting for transfers between devices  322 us (49%)
  other arithmetic  138 us (21%)
  local copies, waits for them, and re-layouts  84.1 us (13%)
  matrix products  39.5 us (6%)
  blocking collectives  23.7 us (4%)
  between operations  17.3 us (3%)
  starting transfers between devices  17.1 us (3%)
    reduce_scatter x1, waiting for transfers between devices, on_device(): lax.psum_scatter(jnp.einsum('td,tsc->dsc', tokens, grad_mixed, preferred_...  160 us
    another operation x130, local copies, waits for them, and re-layouts, tap_sums(): return jnp.stack(pieces, 0)  69.7 us
    all_gather x1, waiting for transfers between devices, on_device(): gathered = lax.all_gather(w_in, 'ctx', axis=0, tiled=True)  54.6 us
    reduce_sum x17, other arithmetic, tap_sums(): pieces.append(jnp.sum(grads * ext[first:first + count] * keep_mask, axis=0))  52.4 us
    another operation x4, other arithmetic, on_device(): jnp.stack([first_grad, grad_product * filtered[:, 2], grad_product * filt...  47.7 us
    all_to_all x1, waiting for transfers between devices, on_device(): lax.all_to_all(loaded, 'ctx', split_axis=1, concat_axis=0, tiled=True)  34 us
    psum x1, waiting for transfers between devices, on_device(): lax.psum(long_local.astype(jnp.bfloat16), 'ctx').astype(jnp.float32)  31.4 us
    ppermute x3, waiting for transfers between devices, on_device(): lax.ppermute(ring[-1], 'fsdp', [(dev, (dev + 1) % 4) for dev in range(4)])  26.8 us
  transfers between devices with their start and end apart: 12, of which 9 were waited for; matrix products, arithmetic and copies ran while one was open for 31% of the time, Pallas kernels for 0%

profile of v1, /device:TPU:0, one launch (start us, length us, event | category | flops | bytes accessed | tf_op | source)
XLA Modules:
  0.0 641.2 jit_solution(2201271811482145461)
XLA Ops:
  7.9 5.3 all-to-all-start
  19.6 34.0 %all-to-all-done = bf16[1,8,128,1024]{3,2,0,1:T(8,128)(2,1)S(1)} async-done(((bf16[1,8,128,1024]{3,2,0,1:T(8,128)(2,1)}), bf16[1,8,128,1024]{3,2,0,1:T(8,128)(2,1)S(1)}, u32[]{:S(2)}, u32[]{:S(2)}) %all-to-all-start) | async-done | bytes 2097184 | tf_op jit(solution)/shard_map/all_to_all | solution.py:59
  57.5 9.0 %collective-permute-done = bf16[256,1024]{1,0:T(8,128)(2,1)S(1)} collective-permute-done((bf16[256,1024]{1,0:T(8,128)(2,1)S(1)}, bf16[256,1024]{1,0:T(8,128)(2,1)S(1)}, u32[]{:S(2)}, u32[]{:S(2)}) %collective-permute-start) | collective-permute-done | bytes 524320 | tf_op jit(solution)/shard_map/ppermute | solution.py:72
  68.6 10.0 %collective-permute-done.1 = bf16[256,1024]{1,0:T(8,128)(2,1)S(1)} collective-permute-done((bf16[256,1024]{1,0:T(8,128)(2,1)S(1)}, bf16[256,1024]{1,0:T(8,128)(2,1)S(1)}, u32[]{:S(2)}, u32[]{:S(2)}) %collective-permute-start.1) | collective-permute-done | bytes 524320 | tf_op jit(solution)/shard_map/ppermute | solution.py:72
  81.8 7.8 %collective-permute-done.2 = bf16[256,1024]{1,0:T(8,128)(2,1)S(1)} collective-permute-done((bf16[256,1024]{1,0:T(8,128)(2,1)S(1)}, bf16[256,1024]{1,0:T(8,128)(2,1)S(1)}, u32[]{:S(2)}, u32[]{:S(2)}) %collective-permute-start.2) | collective-permute-done | bytes 524320 | tf_op jit(solution)/shard_map/ppermute | solution.py:72
  96.6 54.6 %all-gather.2.cloned.1.call-done = bf16[4096,3,1024]{2,0,1:T(8,128)(2,1)} async-done(((bf16[512,3,1024]{2,0,1:T(8,128)(2,1)}), bf16[4096,3,1024]{2,0,1:T(8,128)(2,1)}) %all-gather.2.cloned.1.call-update) | async-done | bytes 25165840 | tf_op jit(solution)/shard_map/all_gather | solution.py:76
  151.2 12.2 %fusion.34 = bf16[256,3,1024]{2,0,1:T(8,128)(2,1)S(1)} fusion(bf16[4096,3,1024]{2,0,1:T(8,128)(2,1)} %all-gather.2.cloned.1.call-done, bf16[256,8192]{1,0:T(8,128)(2,1)} %constant_dynamic-update-slice_fusion, s32[]{:T(128)S(6)} %select_n.26), kind=kOutput, calls=%fused_computation.179 | convolution fusion | flops 6443237376 | bytes 28835844 | tf_op jit(solution)/shard_map/td,dsc->tsc/dot_general | solution.py:77
  167.0 3.6 multiply_add_fusion
  170.9 3.7 collective-permute-start.4
  176.1 3.4 fusion.268
  181.8 3.3 fusion.270
  185.1 3.3 fusion.272
  188.4 3.3 fusion.274
  191.7 3.3 fusion.276
  204.6 3.3 fusion.284
  211.3 3.3 fusion.288
  214.7 3.5 fusion.290
  218.6 3.3 fusion.292
  222.3 9.1 %multiply_add_fusion.2 = f32[256,1024]{1,0:T(8,128)S(1)} fusion(f32[383,1024]{1,0:T(8,128)S(1)} %maximum_convert_fusion.2, f32[256]{0:T(256)} %copy-done.108, f32[1024]{0:T(1024)S(1)} %bitcast.308, f32[256]{0:T(256)} %copy-done.109, f32[1024]{0:T(1024)S(1)} %bitcast.311, f32[256]{0:T(256)} %copy-done.110, f32[1024]{0:T(1024)S(1)} %bitcast.313, ...), kind=kLoop, calls=%fused_computation.834 | loop fusion | flops 33554432 | bytes 46357504 | tf_op jit(solution)/shard_map/add | solution.py:28
  231.4 19.1 %fusion.552 = (bf16[256,1,1024]{2,0,1:T(8,128)(2,1)}, f32[256,1024]{1,0:T(8,128)}) fusion(bf16[256,1024]{1,0:T(8,128)(2,1)} %param.13, f32[256]{0:T(256)} %get-tuple-element.435, f32[383,1024]{1,0:T(8,128)S(1)} %maximum_convert_fusion.2, f32[1024]{0:T(1024)} %bitcast.278, f32[256]{0:T(256)} %get-tuple-element.436, f32[1024]{0:T(1024)} %bitcast.280, ...), kind=kLoop, calls=%fused_computation.842 | loop fusion | flops 67633152 | bytes 92709888 | tf_op jit(solution)/shard_map/stack | solution.py:101
  255.5 8.4 %fusion.488 = f32[256,1024]{1,0:T(8,128)} fusion(f32[383,1024]{1,0:T(8,128)S(1)} %maximum_convert_fusion.3, f32[256]{0:T(256)} %get-tuple-element.407, f32[256]{0:T(256)} %get-tuple-element.408, f32[256]{0:T(256)} %get-tuple-element.409, f32[256]{0:T(256)} %get-tuple-element.410, f32[256]{0:T(256)} %get-tuple-element.411, f32[256]{0:T(256)} %get-tuple-element.412, ...), kind=kLoop, calls=%fused_computation.734 | loop fusion | flops 24903680 | bytes 34766848 | tf_op jit(solution)/shard_map/add | solution.py:43
  264.1 25.0 %fusion.550 = (bf16[256,1,1024]{2,0,1:T(8,128)(2,1)}, f32[256,1024]{1,0:T(8,128)}) fusion(f32[256,3,1024]{2,0,1:T(8,128)} %copy-done.4, f32[256]{0:T(256)} %get-tuple-element.307, f32[383,1024]{1,0:T(8,128)S(1)} %maximum_convert_fusion.3, f32[1024]{0:T(1024)S(1)} %bitcast.279, f32[256]{0:T(256)} %get-tuple-element.308, f32[1024]{0:T(1024)S(1)} %bitcast.281, ...), kind=kLoop, calls=%fused_computation.840 | loop fusion | flops 76021760 | bytes 104824832 | tf_op jit(solution)/shard_map/stack | solution.py:101
  289.1 3.4 fusion.551
  354.7 10.6 %stack.704 = bf16[128,1024]{1,0:T(8,128)(2,1)} concatenate(bf16[1,1024]{1,0:T(2,128)(2,1)S(1)} %stack.576, bf16[1,1024]{1,0:T(2,128)(2,1)S(1)} %stack.577, bf16[1,1024]{1,0:T(2,128)(2,1)S(1)} %stack.578, bf16[1,1024]{1,0:T(2,128)(2,1)S(1)} %stack.579, bf16[1,1024]{1,0:T(2,128)(2,1)S(1)} %stack.580, bf16[1,1024]{1,0:T(2,128)(2,1)S(1)} %stack.581, bf16[1,1024]{1,0:T(2,128)(2,1)S(1)} %stack.582, ...), dimensions={0} | concatenate | bytes 524288 | tf_op jit(solution)/shard_map/stack | solution.py:55
  365.9 3.9 fusion.17
  369.8 13.2 %fusion = bf16[256,4096]{1,0:T(8,128)(2,1)} fusion(bf16[256,3,1024]{2,0,1:T(8,128)(2,1)S(1)} %fusion.17, bf16[4096,3,1024]{2,0,1:T(8,128)(2,1)} %all-gather.2.cloned.1.call-done), kind=kOutput, calls=%fused_computation.137 | convolution fusion | flops 6443499520 | bytes 28835840 | tf_op jit(solution)/shard_map/tsc,dsc->td/dot_general | solution.py:132
  383.0 13.5 %convolution_convert_fusion = bf16[4096,3,1024]{2,0,1:T(8,128)(2,1)} fusion(bf16[256,3,1024]{2,0,1:T(8,128)(2,1)S(1)} %fusion.17, bf16[256,8192]{1,0:T(8,128)(2,1)} %constant_dynamic-update-slice_fusion, s32[]{:T(128)S(6)} %select_n.26), kind=kOutput, calls=%fused_computation.128 | convolution fusion | flops 6455033856 | bytes 28835844 | tf_op jit(solution)/shard_map/td,tsc->dsc/dot_general | solution.py:139
  396.6 31.4 %all-reduce.2.cloned.1.call-done = bf16[128,1024]{1,0:T(8,128)(2,1)} async-done(((bf16[128,1024]{1,0:T(8,128)(2,1)}), bf16[128,1024]{1,0:T(8,128)(2,1)}) %all-reduce.2.cloned.1.call-update) | async-done | bytes 262160 | tf_op jit(solution)/shard_map/psum | solution.py:130
  432.0 3.7 fusion.14
  435.9 23.7 %psum.14 = bf16[3,7,1024]{2,0,1:T(4,128)(2,1)S(1)} all-reduce(bf16[3,7,1024]{2,0,1:T(4,128)(2,1)S(1)} %bitcast.213), channel_id=1, replica_groups=mesh['ctx'=8,'fsdp'=4] {'ctx'}, use_global_device_ids=true, to_apply=%region_13.14 | all-reduce | flops 21504 | bytes 86016 | tf_op jit(solution)/shard_map/psum | solution.py:127
  460.2 14.0 %reduce-scatter.3.cloned.1.call-done = bf16[256,1024]{1,0:T(8,128)(2,1)} async-done(((bf16[256,4096]{1,0:T(8,128)(2,1)}), bf16[256,1024]{1,0:T(8,128)(2,1)}) %reduce-scatter.3.cloned.1.call-update) | async-done | bytes 524304 | tf_op jit(solution)/shard_map/reduce_scatter | solution.py:135
  474.2 160.3 %reduce-scatter.5.cloned.1.call-done = bf16[512,3,1024]{2,0,1:T(8,128)(2,1)} async-done(((bf16[4096,3,1024]{2,0,1:T(8,128)(2,1)}), bf16[512,3,1024]{2,0,1:T(8,128)(2,1)}) %reduce-scatter.5.cloned.1.call-update) | async-done | bytes 3145744 | tf_op jit(solution)/shard_map/reduce_scatter | solution.py:138
  (583 shorter events, 114.5 us)
Async XLA Ops:
  7.2 144.0 %all-gather.2.cloned.1.call-start = ((), (), s32[]{:S(2)}) async-start(), calls=%async_computation.3 | async-start | bytes 28311552 | tf_op jit(solution)/shard_map/all_gather | solution.py:76
  7.9 45.7 %all-to-all-start = ((bf16[1,8,128,1024]{3,2,0,1:T(8,128)(2,1)}), bf16[1,8,128,1024]{3,2,0,1:T(8,128)(2,1)S(1)}, u32[]{:S(2)}, u32[]{:S(2)}) async-start(bf16[1,8,128,1024]{3,2,0,1:T(8,128)(2,1)} %bitcast.2), calls=%async_computation | async-start | bytes 4194304 | tf_op jit(solution)/shard_map/all_to_all | solution.py:59
  13.3 414.7 %all-reduce.2.cloned.1.call-start = ((), (), s32[]{:S(2)}) async-start(), calls=%async_computation.6 | async-start | bytes 524288 | tf_op jit(solution)/shard_map/psum | solution.py:130
  54.4 12.2 %collective-permute-start = (bf16[256,1024]{1,0:T(8,128)(2,1)S(1)}, bf16[256,1024]{1,0:T(8,128)(2,1)S(1)}, u32[]{:S(2)}, u32[]{:S(2)}) collective-permute-start(bf16[256,1024]{1,0:T(8,128)(2,1)S(1)} %convolution_convert_fusion.1), channel_id=1, source_target_pairs={{0,1},{1,2},{2,3},{3,0},{4,5},{5,6},{6,7},{7,4},{8,9},{9,10},{10,1... | collective-permute-start | bytes 1572872 | tf_op jit(solution)/shard_map/ppermute | solution.py:72
  66.5 12.1 %collective-permute-start.1 = (bf16[256,1024]{1,0:T(8,128)(2,1)S(1)}, bf16[256,1024]{1,0:T(8,128)(2,1)S(1)}, u32[]{:S(2)}, u32[]{:S(2)}) collective-permute-start(bf16[256,1024]{1,0:T(8,128)(2,1)S(1)} %collective-permute-done), channel_id=1, source_target_pairs={{0,1},{1,2},{2,3},{3,0},{4,5},{5,6},{6,7},{7,4},{8,9},{9,10},{10,1... | collective-permute-start | bytes 1572872 | tf_op jit(solution)/shard_map/ppermute | solution.py:72
  78.6 11.0 %collective-permute-start.2 = (bf16[256,1024]{1,0:T(8,128)(2,1)S(1)}, bf16[256,1024]{1,0:T(8,128)(2,1)S(1)}, u32[]{:S(2)}, u32[]{:S(2)}) collective-permute-start(bf16[256,1024]{1,0:T(8,128)(2,1)S(1)} %collective-permute-done.1), channel_id=1, source_target_pairs={{0,1},{1,2},{2,3},{3,0},{4,5},{5,6},{6,7},{7,4},{8,9},{9,10},{10,1... | collective-permute-start | bytes 1572872 | tf_op jit(solution)/shard_map/ppermute | solution.py:72
  81.5 126.5 %copy-start.110 = (f32[256]{0:T(256)}, f32[256]{0:T(256)S(1)}, u32[]{:S(2)}) copy-start(f32[256]{0:T(256)S(1)} %get-tuple-element.521) | copy-start | bytes 3076
  81.6 129.7 %copy-start.118 = (f32[256]{0:T(256)}, f32[256]{0:T(256)S(1)}, u32[]{:S(2)}) copy-start(f32[256]{0:T(256)S(1)} %get-tuple-element.529) | copy-start | bytes 3076
  81.6 129.7 %copy-start.119 = (f32[256]{0:T(256)}, f32[256]{0:T(256)S(1)}, u32[]{:S(2)}) copy-start(f32[256]{0:T(256)S(1)} %get-tuple-element.530) | copy-start | bytes 3076
  81.6 129.7 %copy-start.120 = (f32[256]{0:T(256)}, f32[256]{0:T(256)S(1)}, u32[]{:S(2)}) copy-start(f32[256]{0:T(256)S(1)} %get-tuple-element.531) | copy-start | bytes 3076
  81.6 129.7 %copy-start.121 = (f32[256]{0:T(256)}, f32[256]{0:T(256)S(1)}, u32[]{:S(2)}) copy-start(f32[256]{0:T(256)S(1)} %get-tuple-element.532) | copy-start | bytes 3076
  81.6 129.7 %copy-start.122 = (f32[256]{0:T(256)}, f32[256]{0:T(256)S(1)}, u32[]{:S(2)}) copy-start(f32[256]{0:T(256)S(1)} %get-tuple-element.533) | copy-start | bytes 3076
  81.6 129.7 %copy-start.123 = (f32[256]{0:T(256)}, f32[256]{0:T(256)S(1)}, u32[]{:S(2)}) copy-start(f32[256]{0:T(256)S(1)} %get-tuple-element.534) | copy-start | bytes 3076
  81.6 129.7 %copy-start.124 = (f32[256]{0:T(256)}, f32[256]{0:T(256)S(1)}, u32[]{:S(2)}) copy-start(f32[256]{0:T(256)S(1)} %get-tuple-element.535) | copy-start | bytes 3076
  81.6 129.7 %copy-start.125 = (f32[256]{0:T(256)}, f32[256]{0:T(256)S(1)}, u32[]{:S(2)}) copy-start(f32[256]{0:T(256)S(1)} %get-tuple-element.536) | copy-start | bytes 3076
  81.6 133.0 %copy-start.126 = (f32[256]{0:T(256)}, f32[256]{0:T(256)S(1)}, u32[]{:S(2)}) copy-start(f32[256]{0:T(256)S(1)} %get-tuple-element.537) | copy-start | bytes 3076
  81.7 133.0 %copy-start.127 = (f32[256]{0:T(256)}, f32[256]{0:T(256)S(1)}, u32[]{:S(2)}) copy-start(f32[256]{0:T(256)S(1)} %get-tuple-element.538) | copy-start | bytes 3076
  81.7 133.0 %copy-start.128 = (f32[256]{0:T(256)}, f32[256]{0:T(256)S(1)}, u32[]{:S(2)}) copy-start(f32[256]{0:T(256)S(1)} %get-tuple-element.539) | copy-start | bytes 3076
  81.7 133.0 %copy-start.129 = (f32[256]{0:T(256)}, f32[256]{0:T(256)S(1)}, u32[]{:S(2)}) copy-start(f32[256]{0:T(256)S(1)} %get-tuple-element.540) | copy-start | bytes 3076
  81.7 133.0 %copy-start.130 = (f32[256]{0:T(256)}, f32[256]{0:T(256)S(1)}, u32[]{:S(2)}) copy-start(f32[256]{0:T(256)S(1)} %get-tuple-element.541) | copy-start | bytes 3076
  81.7 133.0 %copy-start.131 = (f32[256]{0:T(256)}, f32[256]{0:T(256)S(1)}, u32[]{:S(2)}) copy-start(f32[256]{0:T(256)S(1)} %get-tuple-element.542) | copy-start | bytes 3076
  81.7 133.0 %copy-start.132 = (f32[256]{0:T(256)}, f32[256]{0:T(256)S(1)}, u32[]{:S(2)}) copy-start(f32[256]{0:T(256)S(1)} %get-tuple-element.543) | copy-start | bytes 3076
  81.7 133.0 %copy-start.133 = (f32[256]{0:T(256)}, f32[256]{0:T(256)S(1)}, u32[]{:S(2)}) copy-start(f32[256]{0:T(256)S(1)} %get-tuple-element.544) | copy-start | bytes 3076
  81.7 136.5 %copy-start.134 = (f32[256]{0:T(256)}, f32[256]{0:T(256)S(1)}, u32[]{:S(2)}) copy-start(f32[256]{0:T(256)S(1)} %get-tuple-element.545) | copy-start | bytes 3076
  81.7 136.5 %copy-start.135 = (f32[256]{0:T(256)}, f32[256]{0:T(256)S(1)}, u32[]{:S(2)}) copy-start(f32[256]{0:T(256)S(1)} %get-tuple-element.546) | copy-start | bytes 3076
  81.7 136.5 %copy-start.136 = (f32[256]{0:T(256)}, f32[256]{0:T(256)S(1)}, u32[]{:S(2)}) copy-start(f32[256]{0:T(256)S(1)} %get-tuple-element.547) | copy-start | bytes 3076
  163.4 3.0 collective-permute-start.3
  170.9 5.0 collective-permute-start.4
  180.3 73.6 %collective-permute-start.5 = (bf16[127,1024]{1,0:T(8,128)(2,1)}, bf16[127,1024]{1,0:T(8,128)(2,1)S(1)}, u32[]{:S(2)}, u32[]{:S(2)}) collective-permute-start(bf16[127,1024]{1,0:T(8,128)(2,1)} %slice.2608), channel_id=1, source_target_pairs={{4,0},{8,4},{12,8},{16,12},{20,16},{24,20},{28,24},{5,1},{9,5},{13... | collective-permute-start | bytes 780296 | tf_op jit(solution)/shard_map/ppermute | solution.py:10
  293.1 72.3 %collective-permute-start.6 = (bf16[6,3,1024]{2,0,1:T(8,128)(2,1)S(1)}, bf16[6,3,1024]{2,0,1:T(8,128)(2,1)S(1)}, u32[]{:S(2)}, u32[]{:S(2)}) collective-permute-start(bf16[6,3,1024]{2,0,1:T(8,128)(2,1)S(1)} %slice.2737), channel_id=1, source_target_pairs={{4,0},{8,4},{12,8},{16,12},{20,16},{24,20},{28,24},{5,1},{9,5},{13... | collective-permute-start | bytes 110600 | tf_op jit(solution)/shard_map/ppermute | solution.py:10
  365.4 108.8 %reduce-scatter.3.cloned.1.call-start = ((), (), s32[]{:S(2)}) async-start(), calls=%async_computation.4 | async-start | bytes 2621440 | tf_op jit(solution)/shard_map/reduce_scatter | solution.py:135
  383.0 251.5 %reduce-scatter.5.cloned.1.call-start = ((), (), s32[]{:S(2)}) async-start(), calls=%async_computation.5 | async-start | bytes 28311552 | tf_op jit(solution)/shard_map/reduce_scatter | solution.py:138
  (165 other events, 4928.8 us)
Sparse Core Ops, SparseCore 0:
  9.9 141.2 all-gather.1
  365.5 62.3 all-reduce.1
  430.9 43.2 reduce-scatter.2
  478.2 156.1 reduce-scatter.4
